TPU v7x, 256 devices: a whole 4x4x8 slice. The times are simulated.
256 devices in a mesh: ctx: 16 (over y, x), tp: 16 (over z, core).
Axes of the slice: x: 4, y: 4, z: 8, core: 2. Of those that a mesh axis runs over, the one named last changes fastest.
Arguments:
- residual: bfloat16 [2048, 6144], P('ctx', 'tp'), may hold values from -65 to 65
- query_rows: bfloat16 [2048, 8192], P('ctx', 'tp'), may hold values from -6 to 6
- key_rows: bfloat16 [2048, 8192], P('ctx', 'tp'), may hold values from -6 to 6
- value_rows: bfloat16 [2048, 8192], P('ctx', 'tp'), may hold values from -6 to 6
- head_rates: float32 [64], replicated, may hold values from 0 to 1
- doc_lengths: int32 [4], replicated, may hold values from 1 to 1024, 2048 in all
- attn_gain: float32 [8192], P('tp'), may hold values from 0.1 to 1.9
- out_weight: bfloat16 [8192, 6144], P('tp', 'ctx'), may hold values from -0.09375 to 0.09375
- moe_gain: float32 [6144], P('tp'), may hold values from 0.1 to 1.9
- expert_ids: int32 [2048, 2], P('ctx'), may hold values from 0 to 15, all different within a row; in each aligned block of 128 rows (0 to 127, 128 to 255, ...) at most 24 rows name the same one
- expert_weights: float32 [2048, 2], P('ctx'), may hold values from 0.2 to 1
- gate_weight: bfloat16 [16, 6144, 4608], P('ctx', None, 'tp'), may hold values from -0.078125 to 0.078125
- up_weight: bfloat16 [16, 6144, 4608], P('ctx', None, 'tp'), may hold values from -0.078125 to 0.078125
- down_weight: bfloat16 [16, 4608, 6144], P('ctx', 'tp'), may hold values from -0.125 to 0.125
Outputs:
- output: bfloat16 [2048, 6144], P('ctx', 'tp')
Inputs may be any that keep to these rules, and one draw needn't show every extreme that they name: `expert_ids`: each token names 2 different experts; among the tokens of one device (aligned blocks of 128 rows) no expert is named more than 24 times, a bound that some block reaches. `doc_lengths`: the longest document holds exactly 1024 positions.
All inputs are finite; a program needn't handle non-finite values.
Results may differ from a plain program's by a relative error of at most 0.015.
Values may be sent and summed in bfloat16 or wider, within the bound.
A program may use at most 64 MiB of HBM per device.

v0:
```python
import jax
import jax.numpy as jnp
from jax import lax
from jax.sharding import Mesh
from jax.sharding import PartitionSpec as P

D = 6144
HD = 128
TOP = 2
CTX = ("ctx_0", "ctx_1")
TP = ("tp_0", "tp_1")


def nothing_yet(x, identity):
    return jax.tree.map(
        lambda part, zero: jnp.zeros_like(part) + jnp.asarray(zero, part.dtype), x, identity
    )


def carried_in(x, axes, combine, identity):
    before = start = nothing_yet(x, identity)
    running = x
    for axis in reversed(axes):
        peers, index = (lax.axis_size(axis), lax.axis_index(axis))
        pieces = jax.tree.map(
            lambda part, kind: lax.all_gather(part.astype(kind), axis),
            running,
            (jnp.bfloat16, jnp.bfloat16),
        )
        inside, running = (start, start)
        for k in range(peers):
            passed = k < index
            running = combine(
                running, jax.tree.map(lambda part, own: part[k].astype(own.dtype), pieces, x)
            )
            inside = jax.tree.map(lambda new, old: jnp.where(passed, new, old), running, inside)
        before = combine(inside, before)
    return before


def cut_along(x, dim, peers):
    lengths = x.shape
    tiles = x.reshape(*lengths[:dim], peers, lengths[dim] // peers, *lengths[dim + 1 :])
    return jnp.moveaxis(tiles, dim, 0)


def sum_at_owner(x, axis, dim):
    peers = lax.axis_size(axis)
    tiles = lax.all_to_all(cut_along(x, dim, peers), axis, 0, 0, tiled=True)
    return jnp.sum(tiles.astype(jnp.float32), axis=0)


def sent_to_all(x, axis):
    peers = lax.axis_size(axis)
    return lax.all_to_all(jnp.broadcast_to(x[None], (peers, *x.shape)), axis, 0, 0, tiled=True)


def taken_together(x, axis):
    return sent_to_all(x, axis).sum(axis=0)


def summed_rows(x, chips, core, dim):
    sizes = (lax.axis_size(chips), lax.axis_size(core))
    tiles = cut_along(x, dim, sizes[0] * sizes[1])
    inside = tiles.shape[1:]
    tiles = tiles.reshape(*sizes, *inside).swapaxes(0, 1).reshape(-1, *inside)
    tiles = lax.psum_scatter(tiles, core, scatter_dimension=0, tiled=True)
    return lax.psum_scatter(tiles, chips, scatter_dimension=0, tiled=True)[0]


def segment_of(doc_lengths, positions):
    doc_ends = jnp.cumsum(doc_lengths)
    doc_starts = doc_ends - doc_lengths
    return jnp.sum((positions[:, None] >= doc_starts[None, :]).astype(jnp.int32), axis=1) - 1


def local_attention(query_h, key_h, value_h, head_decay, segments, seg_before):
    length = query_h.shape[0]
    offsets = jnp.arange(length, dtype=jnp.int32)
    distance = (offsets[:, None] - offsets[None, :]).astype(jnp.float32)
    allowed = (offsets[:, None] >= offsets[None, :]) & (segments[:, None] == segments[None, :])
    decay_mask = jnp.where(
        allowed[None], jnp.exp(-head_decay[:, None, None] * jnp.maximum(distance, 0.0)[None]), 0.0
    )
    scores = jnp.einsum("ihd,jhd->hij", query_h, key_h, preferred_element_type=jnp.float32)
    weights = (scores * decay_mask).astype(jnp.bfloat16)
    within = jnp.einsum("hij,jhd->ihd", weights, value_h, preferred_element_type=jnp.float32)
    last_seg = segments[length - 1]
    fading = jnp.where(
        (segments == last_seg)[:, None],
        jnp.exp(-head_decay[None, :] * (length - 1 - offsets).astype(jnp.float32)[:, None]),
        0.0,
    )
    weighted_keys = key_h.astype(jnp.float32) * fading[:, :, None]
    local_state = jnp.einsum(
        "jhd,jhe->hde", weighted_keys, value_h.astype(jnp.float32), precision=lax.Precision.HIGHEST
    )
    carry_factor = jnp.where(last_seg == seg_before, jnp.exp(-head_decay * length), 0.0)
    reaching = jnp.where(
        (segments == seg_before)[:, None],
        jnp.exp(-head_decay[None, :] * (offsets + 1).astype(jnp.float32)[:, None]),
        0.0,
    )
    return (within, local_state, carry_factor, reaching)


def shards(
    residual,
    query_rows,
    key_rows,
    value_rows,
    head_rates,
    doc_lengths,
    attn_gain,
    out_weight,
    moe_gain,
    expert_ids,
    expert_weights,
    gate_weight,
    up_weight,
    down_weight,
):
    length = query_rows.shape[0]
    local_heads = attn_gain.shape[0] // HD
    ctx_index = lax.axis_index(CTX)
    tp_index = lax.axis_index(TP)
    head_decay = lax.dynamic_slice_in_dim(head_rates, tp_index * local_heads, local_heads)
    first_pos = ctx_index * length
    positions = first_pos + jnp.arange(length, dtype=jnp.int32)
    segments = segment_of(doc_lengths, positions)
    seg_before = segment_of(doc_lengths, jnp.reshape(first_pos - 1, (1,)))[0]
    query_h = query_rows.reshape(length, local_heads, HD)
    key_h = key_rows.reshape(length, local_heads, HD)
    value_h = value_rows.reshape(length, local_heads, HD)
    within, local_state, carry_factor, reaching = local_attention(
        query_h, key_h, value_h, head_decay, segments, seg_before
    )

    def combine(earlier, later_one):
        return (earlier[0] * later_one[0], later_one[0][:, None, None] * earlier[1] + later_one[1])

    prefix = carried_in(
        (carry_factor, local_state),
        CTX,
        combine,
        (jnp.ones_like(carry_factor), jnp.zeros_like(local_state)),
    )
    incoming = prefix[1]
    inter = (
        jnp.einsum(
            "ihd,hde->ihe", query_h.astype(jnp.float32), incoming, precision=lax.Precision.HIGHEST
        )
        * reaching[:, :, None]
    )
    mixed_out = within + inter
    scaled = mixed_out * lax.rsqrt(jnp.mean(mixed_out * mixed_out, axis=-1, keepdims=True) + 1e-06)
    heads_out = (scaled.reshape(length, local_heads * HD) * attn_gain).astype(jnp.bfloat16)
    partial_out = jnp.dot(
        heads_out,
        lax.all_gather(out_weight, CTX, axis=1, tiled=True),
        preferred_element_type=jnp.float32,
    )
    attn_out = sum_at_owner(partial_out.astype(jnp.bfloat16), TP, 1)
    hidden_state = (residual.astype(jnp.float32) + attn_out).astype(jnp.bfloat16)
    widened = hidden_state.astype(jnp.float32)
    sum_squares = taken_together(jnp.sum(widened * widened, axis=1), TP)
    moe_input = (widened * lax.rsqrt(sum_squares / D + 1e-05)[:, None] * moe_gain).astype(
        jnp.bfloat16
    )
    experts = lax.axis_size(CTX)
    capacity = 3 * length * TOP // (2 * experts)
    flat_ids = expert_ids.reshape(-1)
    onehot = (flat_ids[:, None] == jnp.arange(experts, dtype=jnp.int32)[None, :]).astype(jnp.int32)
    slot_ranks = jnp.sum((jnp.cumsum(onehot, axis=0) - onehot) * onehot, axis=1)
    slot_index = flat_ids * capacity + slot_ranks
    source_row = (
        jnp.zeros((experts * capacity,), jnp.int32)
        .at[slot_index]
        .set(jnp.arange(length * TOP, dtype=jnp.int32) // TOP)
    )
    occupied = jnp.zeros((experts * capacity,), jnp.bool_).at[slot_index].set(True)
    picked_rows = jnp.where(
        occupied[:, None], moe_input[source_row], jnp.zeros((), moe_input.dtype)
    )
    arrived = lax.all_gather(
        lax.all_to_all(
            picked_rows.reshape(experts, capacity, moe_input.shape[1]),
            CTX,
            split_axis=0,
            concat_axis=0,
            tiled=True,
        ),
        TP,
        axis=2,
        tiled=True,
    )
    flat_in = arrived.reshape(-1, arrived.shape[2])
    gate_pre = jnp.dot(flat_in, gate_weight[0], preferred_element_type=jnp.float32)
    up_pre = jnp.dot(flat_in, up_weight[0], preferred_element_type=jnp.float32)
    activated = (jax.nn.silu(gate_pre) * up_pre).astype(jnp.bfloat16)
    down_term = jnp.dot(activated, down_weight[0], preferred_element_type=jnp.float32)
    reduced = summed_rows(down_term.astype(jnp.bfloat16), "tp_0", "tp_1", 1).astype(jnp.float32)
    outbound = reduced.astype(jnp.bfloat16).reshape(
        arrived.shape[0], arrived.shape[1], reduced.shape[1]
    )
    returned = lax.all_to_all(outbound, CTX, split_axis=0, concat_axis=0, tiled=True)
    returned_flat = returned.reshape(experts * capacity, returned.shape[2])
    gathered_out = (
        returned_flat[slot_index].reshape(length, TOP, returned.shape[2]).astype(jnp.float32)
    )
    mixture = jnp.sum(gathered_out * expert_weights[:, :, None], axis=1)
    return (widened + mixture).astype(jnp.bfloat16)


def solution(mesh):
    finer = Mesh(mesh.devices.reshape(4, 4, 8, 2), ("ctx_0", "ctx_1", "tp_0", "tp_1"))
    placed = (
        P(CTX, TP),
        P(CTX, TP),
        P(CTX, TP),
        P(CTX, TP),
        P(),
        P(),
        P(TP),
        P(TP, CTX),
        P(TP),
        P(CTX, None),
        P(CTX, None),
        P(CTX, None, TP),
        P(CTX, None, TP),
        P(CTX, TP, None),
    )
    return jax.shard_map(shards, mesh=finer, in_specs=placed, out_specs=P(CTX, TP), check_vma=False)
```

profile of v0, /device:TPU:2, one launch (start us, length us, event | category | flops | bytes accessed | tf_op | source)
XLA Modules:
  0.0 320.3 jit_solution(3398791720834157552)
XLA Ops:
  6.5 0.7 all-gather.6.cloned.1.call-update
  7.3 1.1 reduce-window.19
  8.4 1.3 fusion.98
  12.2 1.3 dynamic-slice
  14.2 0.7 fusion.97
  15.1 9.9 %all-reduce = bf16[16]{0:T(256)(128)(2,1)S(1)} all-reduce(bf16[16]{0:T(256)(128)(2,1)S(1)} %dynamic-update-slice), channel_id=2, replica_groups=mesh['ctx_0'=4,'ctx_1'=4,'tp_0'=8,'tp_1'=2] {'ctx_1'}, use_global_device_ids=true, to_apply=%add | all-reduce | flops 16 | bytes 64
  25.1 0.6 broadcast_select_fusion.5
  25.7 8.6 %all-gather.2 = bf16[4,1,4]{2,1,0:T(2,128)(2,1)S(1)} all-gather(bf16[1,1,4]{2,1,0:T(2,128)(2,1)S(1)} %bitcast.205), channel_id=1, replica_groups=mesh['ctx_0'=4,'ctx_1'=4,'tp_0'=8,'tp_1'=2] {'ctx_0'}, dimensions={0}, use_global_device_ids=true | all-gather | bytes 40 | tf_op jit(solution)/shard_map/all_gather | solution.py:26
  34.3 1.7 copy.92
  36.0 0.6 convert_maximum_fusion
  36.6 1.3 broadcast_compare_fusion
  37.9 0.7 exponential_select_fusion
  38.6 1.2 convolution_convert_fusion.2
  39.8 12.2 %all-gather.1 = bf16[16,128,128]{2,1,0:T(8,128)(2,1)S(1)} all-gather(bf16[4,128,128]{2,1,0:T(8,128)(2,1)S(1)} %convolution_convert_fusion.2), channel_id=3, replica_groups=mesh['ctx_0'=4,'ctx_1'=4,'tp_0'=8,'tp_1'=2] {'ctx_1'}, dimensions={0}, use_global_device_ids=true | all-gather | bytes 655360 | tf_op jit(solution)/shard_map/all_gather | solution.py:26
  52.1 0.7 copy-done.1
  53.0 15.7 %all_gather.31 = bf16[4,4,128,128]{3,2,1,0:T(8,128)(2,1)} all-gather(bf16[1,4,128,128]{3,2,1,0:T(8,128)(2,1)S(1)} %fusion.28), channel_id=1, replica_groups=mesh['ctx_0'=4,'ctx_1'=4,'tp_0'=8,'tp_1'=2] {'ctx_0'}, dimensions={0}, use_global_device_ids=true | all-gather | bytes 655360 | tf_op jit(solution)/shard_map/all_gather | solution.py:26
  69.9 0.8 fusion.88
  70.7 2.1 convolution_bitcast_fusion.1
  72.9 2.1 multiply_reduce_fusion.1
  75.1 0.8 fusion.37
  75.8 10.6 %all-gather.6.cloned.1.call-done = bf16[512,6144]{1,0:T(8,128)(2,1)} async-done(((bf16[512,384]{1,0:T(8,128)(2,1)}), bf16[512,6144]{1,0:T(8,128)(2,1)}) %all-gather.6.cloned.1.call-update) | async-done | bytes 6291472 | tf_op jit(solution)/shard_map/all_gather | solution.py:160
  86.4 3.9 %convolution_convert_fusion.1 = bf16[128,6144]{1,0:T(8,128)(2,1)S(1)} fusion(bf16[128,512]{0,1:T(8,128)(2,1)} %fusion.37, bf16[512,6144]{1,0:T(8,128)(2,1)} %all-gather.6.cloned.1.call-done), kind=kOutput, calls=%fused_computation.5 | convolution fusion | flops 806092800 | bytes 7995392 | tf_op jit(solution)/shard_map/dot_general | solution.py:158
  90.4 1.4 copy.121
  91.7 7.7 %all-to-all-start = ((bf16[16,128,384]{2,1,0:T(8,128)(2,1)}), bf16[16,128,384]{2,1,0:T(8,128)(2,1)}, u32[]{:S(2)}, u32[]{:S(2)}) async-start(bf16[16,128,384]{2,1,0:T(8,128)(2,1)} %bitcast.194), calls=%async_computation | async-start | bytes 3145728 | tf_op jit(solution)/shard_map/all_to_all | solution.py:49
  99.5 0.7 copy.84
  100.2 1.0 eq.77
  101.2 1.6 eq.73
  103.4 1.3 reduce-window.20
  104.7 0.7 slice_reduce_fusion
  105.4 1.2 reduce-window.21
  106.6 1.2 slice.75
  107.8 1.3 broadcast_multiply_fusion.1
  109.1 1.4 copy.83
  110.5 1.6 mul.332
  112.6 0.8 fusion.91
  113.4 0.7 compare_select_fusion
  114.1 1.6 scatter_custom_fusion.1
  115.7 21.7 %all-to-all-done = bf16[16,128,384]{2,1,0:T(8,128)(2,1)} async-done(((bf16[16,128,384]{2,1,0:T(8,128)(2,1)}), bf16[16,128,384]{2,1,0:T(8,128)(2,1)}, u32[]{:S(2)}, u32[]{:S(2)}) %all-to-all-start) | async-done | bytes 1572896 | tf_op jit(solution)/shard_map/all_to_all | solution.py:49
  137.4 1.6 convert_reduce_fusion
  139.0 1.6 fusion.47
  141.2 4.8 %all-to-all-start.1 = ((f32[16,1,128]{2,1,0:T(1,128)}), f32[16,1,128]{2,1,0:T(1,128)S(1)}, u32[]{:S(2)}, u32[]{:S(2)}) async-start(f32[16,1,128]{2,1,0:T(1,128)} %broadcast_in_dim.65), calls=%async_computation.1 | async-start | bytes 16384 | tf_op jit(solution)/shard_map/all_to_all | solution.py:55
  146.1 2.1 scatter_custom_fusion
  148.2 0.7 broadcast_in_dim.63
  148.9 4.7 %all-to-all-done.1 = f32[16,1,128]{2,1,0:T(1,128)S(1)} async-done(((f32[16,1,128]{2,1,0:T(1,128)}), f32[16,1,128]{2,1,0:T(1,128)S(1)}, u32[]{:S(2)}, u32[]{:S(2)}) %all-to-all-start.1) | async-done | bytes 8224 | tf_op jit(solution)/shard_map/all_to_all | solution.py:55
  154.2 0.7 add_rsqrt_fusion.1
  154.9 1.6 fusion.49
  156.5 3.3 %gather_fusion = bf16[384,384]{1,0:T(8,128)(2,1)} fusion(bf16[128,384]{1,0:T(8,128)(2,1)} %fusion.49, s32[1024]{0:T(1024)S(1)} %pad_clamp_fusion.1), kind=kCustom, calls=%fused_computation | custom fusion | bytes 591360 | tf_op jit(solution)/shard_map/gather | solution.py:183
  159.9 1.1 broadcast_select_fusion
  160.9 14.6 %all_to_all.21 = bf16[16,24,384]{2,1,0:T(8,128)(2,1)} all-to-all(bf16[16,24,384]{2,1,0:T(8,128)(2,1)S(1)} %broadcast_select_fusion), channel_id=1, replica_groups=mesh['ctx_0'=4,'ctx_1'=4,'tp_0'=8,'tp_1'=2] {'ctx_0','ctx_1'}, dimensions={0} | all-to-all | bytes 589824 | tf_op jit(solution)/shard_map/all_to_all | solution.py:186
  175.8 37.1 %all-gather.8.cloned.1.call-done = bf16[16,24,6144]{2,1,0:T(8,128)(2,1)} async-done(((bf16[16,24,384]{2,1,0:T(8,128)(2,1)}), bf16[16,24,6144]{2,1,0:T(8,128)(2,1)}) %all-gather.8.cloned.1.call-update) | async-done | bytes 4718608 | tf_op jit(solution)/shard_map/all_gather | solution.py:185
  213.0 5.6 %fusion.3 = f32[384,288]{0,1:T(8,128)S(1)} fusion(bf16[384,6144]{1,0:T(8,128)(2,1)} %bitcast.207, bf16[1,6144,288]{1,2,0:T(8,128)(2,1)} %param.25), kind=kOutput, calls=%fused_computation.10 | convolution fusion | flops 1358954496 | bytes 8699904 | tf_op jit(solution)/shard_map/dot_general | solution.py:198
  218.8 2.0 fusion.8
  220.8 2.9 convolution_convert_fusion
  223.7 0.7 copy.120
  224.4 2.7 copy.89
  227.2 16.7 %reduce-scatter.3.cloned.1.call-done = bf16[8,384,384]{2,1,0:T(8,128)(2,1)} async-done(((bf16[16,384,384]{2,1,0:T(8,128)(2,1)}), bf16[8,384,384]{2,1,0:T(8,128)(2,1)}) %reduce-scatter.3.cloned.1.call-update) | async-done | bytes 2359312 | tf_op jit(solution)/shard_map/reduce_scatter | solution.py:67
  243.9 47.2 %reduce-scatter.5.cloned.1.call-done = bf16[1,384,384]{2,1,0:T(8,128)(2,1)} async-done(((bf16[8,384,384]{2,1,0:T(8,128)(2,1)}), bf16[1,384,384]{2,1,0:T(8,128)(2,1)}) %reduce-scatter.5.cloned.1.call-update) | async-done | bytes 294928 | tf_op jit(solution)/shard_map/reduce_scatter | solution.py:68
  291.1 7.3 %all-to-all-start.3 = ((bf16[16,24,384]{2,1,0:T(8,128)(2,1)}), bf16[16,24,384]{2,1,0:T(8,128)(2,1)}, u32[]{:S(2)}, u32[]{:S(2)}) async-start(bf16[16,24,384]{2,1,0:T(8,128)(2,1)} %bitcast.199), calls=%async_computation.5 | async-start | bytes 589824 | tf_op jit(solution)/shard_map/all_to_all | solution.py:206
  298.4 0.7 copy.90
  299.2 6.9 %all-to-all-done.3 = bf16[16,24,384]{2,1,0:T(8,128)(2,1)} async-done(((bf16[16,24,384]{2,1,0:T(8,128)(2,1)}), bf16[16,24,384]{2,1,0:T(8,128)(2,1)}, u32[]{:S(2)}, u32[]{:S(2)}) %all-to-all-start.3) | async-done | bytes 294944 | tf_op jit(solution)/shard_map/all_to_all | solution.py:206
  306.0 2.8 gather_fusion.1
  308.8 1.9 reshape.435
  310.7 1.5 multiply_reduce_fusion
  312.2 1.6 fusion.50
  (59 shorter events, 6.0 us)
Async XLA Ops:
  6.5 214.3 %copy-start = (bf16[1,288,6144]{2,1,0:T(8,128)(2,1)S(1)}, bf16[1,288,6144]{2,1,0:T(8,128)(2,1)}, u32[]{:S(2)}) copy-start(bf16[1,288,6144]{2,1,0:T(8,128)(2,1)} %param.27) | copy-start | bytes 10616836
  6.5 79.9 %all-gather.6.cloned.1.call-start = ((), (), s32[]{:S(2)}) async-start(), calls=%async_computation.6 | async-start | bytes 6684672 | tf_op jit(solution)/shard_map/all_gather | solution.py:160
  9.8 1.2 copy-start.13
  9.8 0.6 copy-start.10
  14.9 54.4 %copy-start.11 = (f32[4]{0:T(128)}, f32[4]{0:T(128)S(1)}, u32[]{:S(2)}) copy-start(f32[4]{0:T(128)S(1)} %get-tuple-element.10) | copy-start | bytes 52
  25.7 43.6 %copy-start.9 = (f32[4]{0:T(128)}, f32[4]{0:T(128)S(1)}, u32[]{:S(2)}) copy-start(f32[4]{0:T(128)S(1)} %get-tuple-element.16) | copy-start | bytes 52
  52.0 0.8 copy-start.1
  52.1 17.8 %copy-start.6 = (f32[4]{0:T(128)}, f32[4]{0:T(128)S(1)}, u32[]{:S(2)}) copy-start(f32[4]{0:T(128)S(1)} %get-tuple-element.21) | copy-start | bytes 52
  52.1 17.8 %copy-start.7 = (f32[4]{0:T(128)}, f32[4]{0:T(128)S(1)}, u32[]{:S(2)}) copy-start(f32[4]{0:T(128)S(1)} %get-tuple-element.22) | copy-start | bytes 52
  52.1 17.8 %copy-start.8 = (f32[4]{0:T(128)}, f32[4]{0:T(128)S(1)}, u32[]{:S(2)}) copy-start(f32[4]{0:T(128)S(1)} %get-tuple-element.23) | copy-start | bytes 52
  72.9 2.2 copy-start.5
  90.3 9.2 %copy-start.2 = (s32[128,2]{0,1:T(2,128)S(1)}, s32[128,2]{0,1:T(2,128)}, u32[]{:S(2)}) copy-start(s32[128,2]{0,1:T(2,128)} %param.23) | copy-start | bytes 3076
  91.7 45.7 %all-to-all-start = ((bf16[16,128,384]{2,1,0:T(8,128)(2,1)}), bf16[16,128,384]{2,1,0:T(8,128)(2,1)}, u32[]{:S(2)}, u32[]{:S(2)}) async-start(bf16[16,128,384]{2,1,0:T(8,128)(2,1)} %bitcast.194), calls=%async_computation | async-start | bytes 3145728 | tf_op jit(solution)/shard_map/all_to_all | solution.py:49
  114.1 27.1 %copy-start.3 = (s32[256,1]{0,1:T(1,128)}, s32[256,1]{0,1:T(1,128)S(1)}, u32[]{:S(2)}) copy-start(s32[256,1]{0,1:T(1,128)S(1)} %compare_select_fusion) | copy-start | bytes 3076
  141.2 12.4 %all-to-all-start.1 = ((f32[16,1,128]{2,1,0:T(1,128)}), f32[16,1,128]{2,1,0:T(1,128)S(1)}, u32[]{:S(2)}, u32[]{:S(2)}) async-start(f32[16,1,128]{2,1,0:T(1,128)} %broadcast_in_dim.65), calls=%async_computation.1 | async-start | bytes 16384 | tf_op jit(solution)/shard_map/all_to_all | solution.py:55
  146.0 66.9 %all-gather.8.cloned.1.call-start = ((), (), s32[]{:S(2)}) async-start(), calls=%async_computation.7 | async-start | bytes 5013504 | tf_op jit(solution)/shard_map/all_gather | solution.py:185
  175.6 68.3 %reduce-scatter.3.cloned.1.call-start = ((), (), s32[]{:S(2)}) async-start(), calls=%async_computation.8 | async-start | bytes 7077888 | tf_op jit(solution)/shard_map/reduce_scatter | solution.py:67
  213.0 5.6 %copy-start.14 = (bf16[16,24,6144]{2,1,0:T(8,128)(2,1)S(1)}, bf16[16,24,6144]{2,1,0:T(8,128)(2,1)}, u32[]{:S(2)}) copy-start(bf16[16,24,6144]{2,1,0:T(8,128)(2,1)} %all-gather.8.cloned.1.call-done) | copy-start | bytes 14155780
  213.0 5.9 %copy-start.15 = (bf16[1,6144,288]{1,2,0:T(8,128)(2,1)S(1)}, bf16[1,6144,288]{1,2,0:T(8,128)(2,1)}, u32[]{:S(2)}) copy-start(bf16[1,6144,288]{1,2,0:T(8,128)(2,1)} %param.26) | copy-start | bytes 10616836
  227.1 71.3 %copy-start.12 = (f32[128,2]{0,1:T(2,128)S(1)}, f32[128,2]{0,1:T(2,128)}, u32[]{:S(2)}) copy-start(f32[128,2]{0,1:T(2,128)} %param.24) | copy-start | bytes 3076
  227.1 72.0 %copy-start.4 = (s32[256,1]{0,1:T(1,128)S(1)}, s32[256,1]{0,1:T(1,128)}, u32[]{:S(2)}) copy-start(s32[256,1]{0,1:T(1,128)} %copy-done.3) | copy-start | bytes 3076
  227.2 63.9 %reduce-scatter.5.cloned.1.call-start = ((), (), s32[]{:S(2)}) async-start(), calls=%async_computation.9 | async-start | bytes 2654208 | tf_op jit(solution)/shard_map/reduce_scatter | solution.py:68
  291.1 14.9 %all-to-all-start.3 = ((bf16[16,24,384]{2,1,0:T(8,128)(2,1)}), bf16[16,24,384]{2,1,0:T(8,128)(2,1)}, u32[]{:S(2)}, u32[]{:S(2)}) async-start(bf16[16,24,384]{2,1,0:T(8,128)(2,1)} %bitcast.199), calls=%async_computation.5 | async-start | bytes 589824 | tf_op jit(solution)/shard_map/all_to_all | solution.py:206
Sparse Core Ops, SparseCore 0:
  9.7 76.6 all-gather.5
  175.7 37.1 all-gather.7
  227.3 16.5 reduce-scatter.2
  246.3 44.7 reduce-scatter.4
where the time goes:
time: 321 us; the launch traced here: 320 us
  waiting for transfers between devices  146 us (45%)
  blocking collectives  61.2 us (19%)
  local copies, waits for them, and re-layouts  32.1 us (10%)
  other arithmetic  26.2 us (8%)
  starting transfers between devices  20.2 us (6%)
  matrix products  19.8 us (6%)
  between operations  15.3 us (5%)
    reduce_scatter x1, waiting for transfers between devices, summed_rows(): return lax.psum_scatter(tiles, chips, scatter_dimension=0, tiled=True)[0]  47.2 us
    all_gather x1, waiting for transfers between devices, shards(): lax.all_gather(lax.all_to_all(picked_rows.reshape(experts, capacity, moe_...  37.1 us
    all_gather x3, blocking collectives, carried_in(): lax.all_gather(part.astype(kind), axis)  36.6 us
    all_to_all x1, waiting for transfers between devices, sum_at_owner(): tiles = lax.all_to_all(cut_along(x, dim, peers), axis, 0, 0, tiled=True)  21.7 us
    reduce_scatter x1, waiting for transfers between devices, summed_rows(): tiles = lax.psum_scatter(tiles, core, scatter_dimension=0, tiled=True)  16.7 us
    all_to_all x1, blocking collectives, shards(): lax.all_to_all(picked_rows.reshape(experts, capacity, moe_input.shape[1])...  14.6 us
    all_gather x1, waiting for transfers between devices, shards(): lax.all_gather(out_weight, CTX, axis=1, tiled=True)  10.6 us
    unnamed x1, blocking collectives  9.94 us
  transfers between devices with their start and end apart: 7, of which 7 were waited for; matrix products, arithmetic and copies ran while one was open for 12% of the time, Pallas kernels for 0%

commit v1 on v0

--- a/solution.py
+++ b/solution.py
@@ -182,17 +182,21 @@
     picked_rows = jnp.where(
         occupied[:, None], moe_input[source_row], jnp.zeros((), moe_input.dtype)
     )
-    arrived = lax.all_gather(
-        lax.all_to_all(
-            picked_rows.reshape(experts, capacity, moe_input.shape[1]),
-            CTX,
-            split_axis=0,
-            concat_axis=0,
-            tiled=True,
+    raw = lax.all_to_all(
+        picked_rows.reshape(experts, capacity, moe_input.shape[1]),
+        CTX,
+        split_axis=0,
+        concat_axis=0,
+        tiled=True,
+    )
+    so_far_all = []
+    for _ in range(jax.lax.axis_size(TP)):
+        so_far_all.append(raw)
+    arrived = jnp.concatenate(
+        jax.lax.all_to_all(
+            jnp.stack(so_far_all, axis=0), axis_name=TP, split_axis=0, concat_axis=0
         ),
-        TP,
-        axis=2,
-        tiled=True,
+        2,
     )
     flat_in = arrived.reshape(-1, arrived.shape[2])
     gate_pre = jnp.dot(flat_in, gate_weight[0], preferred_element_type=jnp.float32)

time: 321 us -> 391 us (1.22)
  blocking collectives: 61.2 us -> 170 us
  waiting for transfers between devices: 146 us -> 105 us
  local copies, waits for them, and re-layouts: 32.1 us -> 37.3 us
    all_to_all x0 -> x1, blocking collectives: none -> 108 us  [shards(): jax.lax.all_to_all(jnp.stack(so_far_all, axis=0), axis_name=TP, split_axi...]
    all_gather x1 -> x0, waiting for transfers between devices: 37.1 us -> none  [shards(): lax.all_gather(lax.all_to_all(picked_rows.reshape(experts, capacity, moe_...]
  transfers between devices with their start and end apart: 7 -> 6, of which waited for: 7 -> 6; matrix products, arithmetic and copies ran while one was open for 12% -> 10% of each run, Pallas kernels for 0% -> 0%
where the time goes in v1:
time: 391 us; the launch traced here: 390 us
  blocking collectives  170 us (43%)
  waiting for transfers between devices  105 us (27%)
  local copies, waits for them, and re-layouts  37.3 us (10%)
  other arithmetic  26.2 us (7%)
  starting transfers between devices  19.9 us (5%)
  matrix products  16.2 us (4%)
  between operations  15.3 us (4%)
    all_to_all x1, blocking collectives, shards(): jax.lax.all_to_all(jnp.stack(so_far_all, axis=0), axis_name=TP, split_axi...  108 us
    reduce_scatter x1, waiting for transfers between devices, summed_rows(): return lax.psum_scatter(tiles, chips, scatter_dimension=0, tiled=True)[0]  47.1 us
    all_gather x3, blocking collectives, carried_in(): lax.all_gather(part.astype(kind), axis)  36.6 us
    all_to_all x1, waiting for transfers between devices, sum_at_owner(): tiles = lax.all_to_all(cut_along(x, dim, peers), axis, 0, 0, tiled=True)  21.7 us
    all_to_all x1, blocking collectives, shards(): lax.all_to_all(picked_rows.reshape(experts, capacity, moe_input.shape[1])...  14.5 us
    reduce_scatter x1, waiting for transfers between devices, summed_rows(): tiles = lax.psum_scatter(tiles, core, scatter_dimension=0, tiled=True)  13.7 us
    all_gather x1, waiting for transfers between devices, shards(): lax.all_gather(out_weight, CTX, axis=1, tiled=True)  10.6 us
    unnamed x1, blocking collectives  9.94 us
  transfers between devices with their start and end apart: 6, of which 6 were waited for; matrix products, arithmetic and copies ran while one was open for 10% of the time, Pallas kernels for 0%

profile of v1, /device:TPU:2, one launch (start us, length us, event | category | flops | bytes accessed | tf_op | source)
XLA Modules:
  0.0 389.8 jit_solution(14148434395901354257)
XLA Ops:
  6.5 0.7 all-gather.5.cloned.1.call-update
  7.3 1.1 reduce-window.19
  8.4 1.3 fusion.98
  12.2 1.3 dynamic-slice
  14.2 0.7 fusion.97
  15.1 9.9 %all-reduce = bf16[16]{0:T(256)(128)(2,1)S(1)} all-reduce(bf16[16]{0:T(256)(128)(2,1)S(1)} %dynamic-update-slice), channel_id=2, replica_groups=mesh['ctx_0'=4,'ctx_1'=4,'tp_0'=8,'tp_1'=2] {'ctx_1'}, use_global_device_ids=true, to_apply=%add | all-reduce | flops 16 | bytes 64
  25.7 8.6 %all-gather.2 = bf16[4,1,4]{2,1,0:T(2,128)(2,1)S(1)} all-gather(bf16[1,1,4]{2,1,0:T(2,128)(2,1)S(1)} %bitcast.212), channel_id=1, replica_groups=mesh['ctx_0'=4,'ctx_1'=4,'tp_0'=8,'tp_1'=2] {'ctx_0'}, dimensions={0}, use_global_device_ids=true | all-gather | bytes 40 | tf_op jit(solution)/shard_map/all_gather | solution.py:26
  34.3 1.7 copy.95
  36.6 1.3 broadcast_compare_fusion
  38.6 1.2 convolution_convert_fusion.2
  39.8 12.2 %all-gather.1 = bf16[16,128,128]{2,1,0:T(8,128)(2,1)S(1)} all-gather(bf16[4,128,128]{2,1,0:T(8,128)(2,1)S(1)} %convolution_convert_fusion.2), channel_id=3, replica_groups=mesh['ctx_0'=4,'ctx_1'=4,'tp_0'=8,'tp_1'=2] {'ctx_1'}, dimensions={0}, use_global_device_ids=true | all-gather | bytes 655360 | tf_op jit(solution)/shard_map/all_gather | solution.py:26
  52.1 0.7 copy-done.1
  53.0 15.7 %all_gather.28 = bf16[4,4,128,128]{3,2,1,0:T(8,128)(2,1)} all-gather(bf16[1,4,128,128]{3,2,1,0:T(8,128)(2,1)S(1)} %fusion.28), channel_id=1, replica_groups=mesh['ctx_0'=4,'ctx_1'=4,'tp_0'=8,'tp_1'=2] {'ctx_0'}, dimensions={0}, use_global_device_ids=true | all-gather | bytes 655360 | tf_op jit(solution)/shard_map/all_gather | solution.py:26
  69.9 0.8 fusion.88
  70.7 2.1 convolution_bitcast_fusion.1
  72.9 2.1 multiply_reduce_fusion.1
  75.1 0.8 fusion.37
  75.8 10.6 %all-gather.5.cloned.1.call-done = bf16[512,6144]{1,0:T(8,128)(2,1)} async-done(((bf16[512,384]{1,0:T(8,128)(2,1)}), bf16[512,6144]{1,0:T(8,128)(2,1)}) %all-gather.5.cloned.1.call-update) | async-done | bytes 6291472 | tf_op jit(solution)/shard_map/all_gather | solution.py:160
  86.4 3.9 convolution_convert_fusion.1
  90.4 1.4 copy.125
  91.7 7.7 %all-to-all-start = ((bf16[16,128,384]{2,1,0:T(8,128)(2,1)}), bf16[16,128,384]{2,1,0:T(8,128)(2,1)}, u32[]{:S(2)}, u32[]{:S(2)}) async-start(bf16[16,128,384]{2,1,0:T(8,128)(2,1)} %bitcast.199), calls=%async_computation | async-start | bytes 3145728 | tf_op jit(solution)/shard_map/all_to_all | solution.py:49
  99.5 0.7 copy.86
  100.2 1.0 eq.77
  101.2 1.6 eq.73
  103.4 1.3 reduce-window.20
  104.7 0.7 slice_reduce_fusion
  105.4 1.2 reduce-window.21
  106.6 1.2 slice.75
  107.8 1.3 broadcast_multiply_fusion.1
  109.1 1.4 copy.85
  110.5 1.6 mul.332
  112.6 0.8 fusion.91
  113.4 0.7 compare_select_fusion
  114.1 1.6 scatter_custom_fusion.1
  115.7 21.7 %all-to-all-done = bf16[16,128,384]{2,1,0:T(8,128)(2,1)} async-done(((bf16[16,128,384]{2,1,0:T(8,128)(2,1)}), bf16[16,128,384]{2,1,0:T(8,128)(2,1)}, u32[]{:S(2)}, u32[]{:S(2)}) %all-to-all-start) | async-done | bytes 1572896 | tf_op jit(solution)/shard_map/all_to_all | solution.py:49
  137.4 1.6 convert_reduce_fusion
  139.0 1.6 fusion.47
  141.2 4.8 %all-to-all-start.1 = ((f32[16,1,128]{2,1,0:T(1,128)}), f32[16,1,128]{2,1,0:T(1,128)S(1)}, u32[]{:S(2)}, u32[]{:S(2)}) async-start(f32[16,1,128]{2,1,0:T(1,128)} %broadcast_in_dim.65), calls=%async_computation.1 | async-start | bytes 16384 | tf_op jit(solution)/shard_map/all_to_all | solution.py:55
  146.1 2.1 scatter_custom_fusion
  148.2 0.7 broadcast_in_dim.63
  148.9 4.7 %all-to-all-done.1 = f32[16,1,128]{2,1,0:T(1,128)S(1)} async-done(((f32[16,1,128]{2,1,0:T(1,128)}), f32[16,1,128]{2,1,0:T(1,128)S(1)}, u32[]{:S(2)}, u32[]{:S(2)}) %all-to-all-start.1) | async-done | bytes 8224 | tf_op jit(solution)/shard_map/all_to_all | solution.py:55
  154.2 0.7 add_rsqrt_fusion.1
  154.9 1.6 fusion.49
  156.5 3.3 gather_fusion
  159.9 1.1 broadcast_select_fusion
  160.9 14.5 %all_to_all.26 = bf16[16,24,384]{2,1,0:T(8,128)(2,1)S(1)} all-to-all(bf16[16,24,384]{2,1,0:T(8,128)(2,1)S(1)} %broadcast_select_fusion), channel_id=1, replica_groups=mesh['ctx_0'=4,'ctx_1'=4,'tp_0'=8,'tp_1'=2] {'ctx_0','ctx_1'}, dimensions={0} | all-to-all | bytes 589824 | tf_op jit(solution)/shard_map/all_to_all | solution.py:185
  175.5 0.7 stack.2
  176.2 108.5 %all_to_all.27 = bf16[16,16,24,384]{3,2,1,0:T(8,128)(2,1)S(1)} all-to-all(bf16[16,16,24,384]{3,2,1,0:T(8,128)(2,1)S(1)} %stack.2), channel_id=1, replica_groups=mesh['ctx_0'=4,'ctx_1'=4,'tp_0'=8,'tp_1'=2] {'tp_0','tp_1'}, dimensions={0} | all-to-all | bytes 9437184 | tf_op jit(solution)/shard_map/all_to_all | solution.py:196
  284.6 2.8 copy.90
  287.4 1.6 copy.101
  289.4 2.0 fusion.3
  291.5 2.0 fusion.8
  293.5 2.9 convolution_convert_fusion
  296.4 0.7 copy.124
  297.1 2.7 copy.92
  299.8 13.7 %reduce-scatter.3.cloned.1.call-done = bf16[8,384,384]{2,1,0:T(8,128)(2,1)} async-done(((bf16[16,384,384]{2,1,0:T(8,128)(2,1)}), bf16[8,384,384]{2,1,0:T(8,128)(2,1)}) %reduce-scatter.3.cloned.1.call-update) | async-done | bytes 2359312 | tf_op jit(solution)/shard_map/reduce_scatter | solution.py:67
  313.5 47.1 %reduce-scatter.5.cloned.1.call-done = bf16[1,384,384]{2,1,0:T(8,128)(2,1)} async-done(((bf16[8,384,384]{2,1,0:T(8,128)(2,1)}), bf16[1,384,384]{2,1,0:T(8,128)(2,1)}) %reduce-scatter.5.cloned.1.call-update) | async-done | bytes 294928 | tf_op jit(solution)/shard_map/reduce_scatter | solution.py:68
  360.6 7.3 %all-to-all-start.4 = ((bf16[16,24,384]{2,1,0:T(8,128)(2,1)}), bf16[16,24,384]{2,1,0:T(8,128)(2,1)}, u32[]{:S(2)}, u32[]{:S(2)}) async-start(bf16[16,24,384]{2,1,0:T(8,128)(2,1)} %bitcast.206), calls=%async_computation.6 | async-start | bytes 589824 | tf_op jit(solution)/shard_map/all_to_all | solution.py:210
  367.9 0.7 copy.93
  368.7 6.9 %all-to-all-done.4 = bf16[16,24,384]{2,1,0:T(8,128)(2,1)} async-done(((bf16[16,24,384]{2,1,0:T(8,128)(2,1)}), bf16[16,24,384]{2,1,0:T(8,128)(2,1)}, u32[]{:S(2)}, u32[]{:S(2)}) %all-to-all-start.4) | async-done | bytes 294944 | tf_op jit(solution)/shard_map/all_to_all | solution.py:210
  375.5 2.8 gather_fusion.1
  378.3 1.9 reshape.437
  380.2 1.5 multiply_reduce_fusion
  381.7 1.6 fusion.50
  (60 shorter events, 7.8 us)
Async XLA Ops:
  6.5 286.9 %copy-start = (bf16[1,288,6144]{2,1,0:T(8,128)(2,1)S(1)}, bf16[1,288,6144]{2,1,0:T(8,128)(2,1)}, u32[]{:S(2)}) copy-start(bf16[1,288,6144]{2,1,0:T(8,128)(2,1)} %param.27) | copy-start | bytes 10616836
  6.5 79.9 %all-gather.5.cloned.1.call-start = ((), (), s32[]{:S(2)}) async-start(), calls=%async_computation.7 | async-start | bytes 6684672 | tf_op jit(solution)/shard_map/all_gather | solution.py:160
  9.8 1.2 copy-start.13
  9.8 0.6 copy-start.10
  14.9 54.4 %copy-start.11 = (f32[4]{0:T(128)}, f32[4]{0:T(128)S(1)}, u32[]{:S(2)}) copy-start(f32[4]{0:T(128)S(1)} %get-tuple-element.10) | copy-start | bytes 52
  25.7 43.6 %copy-start.9 = (f32[4]{0:T(128)}, f32[4]{0:T(128)S(1)}, u32[]{:S(2)}) copy-start(f32[4]{0:T(128)S(1)} %get-tuple-element.16) | copy-start | bytes 52
  52.0 0.8 copy-start.1
  52.1 17.8 %copy-start.6 = (f32[4]{0:T(128)}, f32[4]{0:T(128)S(1)}, u32[]{:S(2)}) copy-start(f32[4]{0:T(128)S(1)} %get-tuple-element.21) | copy-start | bytes 52
  52.1 17.8 %copy-start.7 = (f32[4]{0:T(128)}, f32[4]{0:T(128)S(1)}, u32[]{:S(2)}) copy-start(f32[4]{0:T(128)S(1)} %get-tuple-element.22) | copy-start | bytes 52
  52.1 17.8 %copy-start.8 = (f32[4]{0:T(128)}, f32[4]{0:T(128)S(1)}, u32[]{:S(2)}) copy-start(f32[4]{0:T(128)S(1)} %get-tuple-element.23) | copy-start | bytes 52
  72.9 2.2 copy-start.5
  90.3 9.2 %copy-start.2 = (s32[128,2]{0,1:T(2,128)S(1)}, s32[128,2]{0,1:T(2,128)}, u32[]{:S(2)}) copy-start(s32[128,2]{0,1:T(2,128)} %param.23) | copy-start | bytes 3076
  91.7 45.7 %all-to-all-start = ((bf16[16,128,384]{2,1,0:T(8,128)(2,1)}), bf16[16,128,384]{2,1,0:T(8,128)(2,1)}, u32[]{:S(2)}, u32[]{:S(2)}) async-start(bf16[16,128,384]{2,1,0:T(8,128)(2,1)} %bitcast.199), calls=%async_computation | async-start | bytes 3145728 | tf_op jit(solution)/shard_map/all_to_all | solution.py:49
  114.1 27.1 %copy-start.3 = (s32[256,1]{0,1:T(1,128)}, s32[256,1]{0,1:T(1,128)S(1)}, u32[]{:S(2)}) copy-start(s32[256,1]{0,1:T(1,128)S(1)} %compare_select_fusion) | copy-start | bytes 3076
  141.2 12.4 %all-to-all-start.1 = ((f32[16,1,128]{2,1,0:T(1,128)}), f32[16,1,128]{2,1,0:T(1,128)S(1)}, u32[]{:S(2)}, u32[]{:S(2)}) async-start(f32[16,1,128]{2,1,0:T(1,128)} %broadcast_in_dim.65), calls=%async_computation.1 | async-start | bytes 16384 | tf_op jit(solution)/shard_map/all_to_all | solution.py:55
  146.0 167.5 %reduce-scatter.3.cloned.1.call-start = ((), (), s32[]{:S(2)}) async-start(), calls=%async_computation.8 | async-start | bytes 7077888 | tf_op jit(solution)/shard_map/reduce_scatter | solution.py:67
  287.4 2.0 copy-start.14
  289.4 2.0 copy-start.15
  299.8 68.1 %copy-start.12 = (f32[128,2]{0,1:T(2,128)S(1)}, f32[128,2]{0,1:T(2,128)}, u32[]{:S(2)}) copy-start(f32[128,2]{0,1:T(2,128)} %param.24) | copy-start | bytes 3076
  299.8 68.9 %copy-start.4 = (s32[256,1]{0,1:T(1,128)S(1)}, s32[256,1]{0,1:T(1,128)}, u32[]{:S(2)}) copy-start(s32[256,1]{0,1:T(1,128)} %copy-done.3) | copy-start | bytes 3076
  299.8 60.8 %reduce-scatter.5.cloned.1.call-start = ((), (), s32[]{:S(2)}) async-start(), calls=%async_computation.9 | async-start | bytes 2654208 | tf_op jit(solution)/shard_map/reduce_scatter | solution.py:68
  360.6 14.9 %all-to-all-start.4 = ((bf16[16,24,384]{2,1,0:T(8,128)(2,1)}), bf16[16,24,384]{2,1,0:T(8,128)(2,1)}, u32[]{:S(2)}, u32[]{:S(2)}) async-start(bf16[16,24,384]{2,1,0:T(8,128)(2,1)} %bitcast.206), calls=%async_computation.6 | async-start | bytes 589824 | tf_op jit(solution)/shard_map/all_to_all | solution.py:210
Sparse Core Ops, SparseCore 0:
  9.7 76.6 all-gather.4
  299.9 13.5 reduce-scatter.2
  316.1 44.4 reduce-scatter.4
